TPU v7x, 32 devices: a whole 2x2x4 slice. The times are simulated.
32 devices in a mesh: frame: 4 (over z), space: 8 (over y, x, core).
Axes of the slice: x: 2, y: 2, z: 4, core: 2. Of those that a mesh axis runs over, the one named last changes fastest.
Arguments:
- latents: bfloat16 [2, 4, 512, 3072], P(None, 'frame', 'space'), may hold values from -6 to 6
- target: bfloat16 [2, 4, 512, 3072], P(None, 'frame', 'space'), may hold values from -6 to 6
- timesteps: int32 [2], replicated, may hold values from 0 to 999
- valid: int32 [2, 2], replicated, may hold values from 1 to 16, as said below
- tile_mask: int32 [2, 16, 16], replicated, may hold values from 0 to 1, as said below
- w_mod: bfloat16 [256, 18432], replicated, may hold values from -0.5 to 0.5
- w_sqkv: bfloat16 [3, 3072, 2048], P(None, None, 'space'), may hold values from -0.109375 to 0.109375
- w_sout: bfloat16 [2048, 3072], P('space'), may hold values from -0.125 to 0.125
- w_tqkv: bfloat16 [3, 3072, 2048], P(None, None, 'frame'), may hold values from -0.109375 to 0.109375
- w_tout: bfloat16 [2048, 3072], P('frame'), may hold values from -0.125 to 0.125
Outputs:
- mixed: bfloat16 [2, 4, 512, 3072], P(None, 'frame', 'space')
- loss: float32 [], replicated
Inputs may be any that keep to these rules, and one draw needn't show every extreme that they name: Each video's valid frame count is 1 to 4 and valid tile count 1 to 16; video 0 is whole. `tile_mask`: entries are 0 or 1, with ones on the diagonal of every video's mask.
All inputs are finite; a program needn't handle non-finite values.
Results may differ from a plain program's by a relative error of at most 0.017.
Values may be sent and summed in bfloat16 or wider, within the bound.
A program may use at most 128 MiB of HBM per device.

v0:
```python
import math
import jax
import jax.numpy as jnp
from jax import lax
from jax.sharding import PartitionSpec as P

HEAD_DIM = 128
FREQ = 256
TILE = 32


def layer_norm(values):
    mean = jnp.mean(values, -1, keepdims=True)
    centred = values - mean
    var = jnp.mean(centred * centred, -1, keepdims=True)
    return centred * lax.rsqrt(var + 1e-06)


def time_embed(timesteps):
    half = FREQ // 2
    freqs = jnp.exp(-math.log(10000.0) * jnp.arange(half, dtype=jnp.float32) / half)
    angles = timesteps.astype(jnp.float32)[:, None] * freqs[None, :]
    return jnp.concatenate([jnp.cos(angles), jnp.sin(angles)], -1).astype(jnp.bfloat16)


def modulate(values, shift, scale):
    return (
        layer_norm(values.astype(jnp.float32)) * (1.0 + scale[:, None, None, :])
        + shift[:, None, None, :]
    ).astype(jnp.bfloat16)


def frame_attention(qkv, count, tiles, heads):
    length = qkv.shape[0]
    cols = heads * HEAD_DIM
    scale = 1.0 / math.sqrt(HEAD_DIM)
    query = jnp.transpose(qkv[:, :cols].reshape(length, heads, HEAD_DIM), (1, 0, 2))
    keys = jnp.transpose(qkv[:, cols : 2 * cols].reshape(length, heads, HEAD_DIM), (1, 0, 2))
    values = jnp.transpose(qkv[:, 2 * cols :].reshape(length, heads, HEAD_DIM), (1, 0, 2))
    tile_ids = jnp.arange(length, dtype=jnp.int32) // TILE
    expanded = jnp.repeat(jnp.repeat(tiles, TILE, axis=0), TILE, axis=1)
    allowed = (expanded == 1) & (tile_ids[None, :] < count) | (
        tile_ids[:, None] == tile_ids[None, :]
    )

    def one_head(parts):
        q_head, k_head, v_head = parts
        scores = (
            lax.dot_general(
                q_head, k_head, (((1,), (1,)), ((), ())), preferred_element_type=jnp.float32
            )
            * scale
        )
        scores = jnp.where(allowed, scores, -1e30)
        top = jnp.max(scores, -1, keepdims=True)
        weights = jnp.exp(scores - top)
        probs = (weights / jnp.sum(weights, -1, keepdims=True)).astype(jnp.bfloat16)
        return jnp.dot(probs, v_head, preferred_element_type=jnp.float32).astype(jnp.bfloat16)

    outs = lax.map(one_head, (query, keys, values))
    return jnp.transpose(outs, (1, 0, 2)).reshape(length, cols)


def temporal_attention(qkv, count, heads):
    frames, places = (qkv.shape[0], qkv.shape[1])
    cols = heads * HEAD_DIM
    scale = 1.0 / math.sqrt(HEAD_DIM)
    query = qkv[..., :cols].reshape(frames, places, heads, HEAD_DIM)
    keys = qkv[..., cols : 2 * cols].reshape(frames, places, heads, HEAD_DIM)
    values = qkv[..., 2 * cols :].reshape(frames, places, heads, HEAD_DIM)
    scores = jnp.einsum("fphd,gphd->phfg", query, keys, preferred_element_type=jnp.float32) * scale
    frame_ids = jnp.arange(frames, dtype=jnp.int32)
    allowed = (frame_ids[None, :] < count) | (frame_ids[:, None] == frame_ids[None, :])
    scores = jnp.where(allowed, scores, -1e30)
    top = jnp.max(scores, -1, keepdims=True)
    weights = jnp.exp(scores - top)
    probs = (weights / jnp.sum(weights, -1, keepdims=True)).astype(jnp.bfloat16)
    outs = jnp.einsum("phfg,gphd->fphd", probs, values, preferred_element_type=jnp.float32).astype(
        jnp.bfloat16
    )
    return outs.reshape(frames, places, cols)


def group_project(attended, w_out, groups):
    rows = attended.shape[0]
    width = w_out.shape[1]
    parts = attended.reshape(rows, groups, -1)
    weights = w_out.reshape(groups, -1, width)
    terms = jnp.einsum("rgc,gcd->rgd", parts, weights, preferred_element_type=jnp.float32).astype(
        jnp.bfloat16
    )
    return jnp.sum(terms.astype(jnp.float32), axis=1)


def shards(latents, target, timesteps, valid, tile_mask, w_mod, w_sqkv, w_sout, w_tqkv, w_tout):
    videos, frames_dev, span_dev, width = latents.shape
    space_count = lax.axis_size("space")
    frame_count = lax.axis_size("frame")
    embed = time_embed(timesteps)
    mod = jnp.dot(embed, w_mod, preferred_element_type=jnp.float32)
    shift_one, scale_one, gate_one, shift_two, scale_two, gate_two = jnp.split(mod, 6, axis=1)
    h_one = modulate(latents, shift_one, scale_one)
    spatial_heads = w_sqkv.shape[2] // HEAD_DIM
    w_flat = jnp.concatenate([w_sqkv[0], w_sqkv[1], w_sqkv[2]], axis=1)
    qkv_space = jnp.dot(
        lax.all_gather(h_one, "space", axis=2, tiled=True),
        w_flat,
        preferred_element_type=jnp.float32,
    ).astype(jnp.bfloat16)
    span = qkv_space.shape[2]
    frames_flat = qkv_space.reshape(videos * frames_dev, span, -1)
    tile_counts = jnp.repeat(valid[:, 1], frames_dev)
    tiles = jnp.repeat(tile_mask, frames_dev, axis=0)

    def per_frame(parts):
        frame_qkv, count, tiles_one = parts
        return frame_attention(frame_qkv, count, tiles_one, spatial_heads)

    spatial_att = lax.map(per_frame, (frames_flat, tile_counts, tiles)).reshape(
        videos, frames_dev, span, -1
    )
    spatial_att = jnp.transpose(spatial_att, (2, 0, 1, 3))
    w_sall = lax.all_gather(w_sout, "space", axis=0, tiled=True)
    own_rows = lax.all_to_all(spatial_att, "space", split_axis=0, concat_axis=3, tiled=True)
    spatial = group_project(
        own_rows.reshape(span_dev * videos * frames_dev, -1), w_sall, space_count
    )
    spatial = spatial.reshape(span_dev, videos, frames_dev, width)
    spatial = jnp.transpose(spatial, (1, 2, 0, 3))
    x_one = (latents.astype(jnp.float32) + gate_one[:, None, None, :] * spatial).astype(
        jnp.bfloat16
    )
    h_two = modulate(x_one, shift_two, scale_two)
    temporal_heads = w_tqkv.shape[2] // HEAD_DIM
    w_tflat = jnp.concatenate([w_tqkv[0], w_tqkv[1], w_tqkv[2]], axis=1)
    qkv_frame = jnp.dot(
        lax.all_gather(h_two, "frame", axis=1, tiled=True),
        w_tflat,
        preferred_element_type=jnp.float32,
    ).astype(jnp.bfloat16)

    def per_video(parts):
        video_qkv, count = parts
        return temporal_attention(video_qkv, count, temporal_heads)

    temporal_att = lax.map(per_video, (qkv_frame, valid[:, 0]))
    temporal_att = jnp.transpose(temporal_att, (1, 0, 2, 3))
    w_tall = lax.all_gather(w_tout, "frame", axis=0, tiled=True)
    own_frames = lax.all_to_all(temporal_att, "frame", split_axis=0, concat_axis=3, tiled=True)
    temporal = group_project(
        own_frames.reshape(frames_dev * videos * span_dev, -1), w_tall, frame_count
    )
    temporal = temporal.reshape(frames_dev, videos, span_dev, width)
    temporal = jnp.transpose(temporal, (1, 0, 2, 3))
    mixed = (x_one.astype(jnp.float32) + gate_two[:, None, None, :] * temporal).astype(jnp.bfloat16)
    diff = mixed.astype(jnp.float32) - target.astype(jnp.float32)
    squares = jnp.mean(diff * diff, -1)
    frame_ids = lax.axis_index("frame") * frames_dev + jnp.arange(frames_dev, dtype=jnp.int32)
    tile_ids = (lax.axis_index("space") * span_dev + jnp.arange(span_dev, dtype=jnp.int32)) // TILE
    mask = (frame_ids[None, :, None] < valid[:, 0][:, None, None]) & (
        tile_ids[None, None, :] < valid[:, 1][:, None, None]
    )
    local_total = jnp.sum(jnp.where(mask, squares, 0.0))
    total = lax.psum(local_total, ("frame", "space"))
    count = jnp.sum(valid[:, 0] * valid[:, 1]).astype(jnp.float32) * TILE
    return (mixed, total / count)


def solution(mesh):
    return jax.shard_map(
        shards,
        mesh=mesh,
        in_specs=(
            P(None, "frame", "space", None),
            P(None, "frame", "space", None),
            P(),
            P(),
            P(),
            P(),
            P(None, None, "space"),
            P("space", None),
            P(None, None, "frame"),
            P("frame", None),
        ),
        out_specs=(P(None, "frame", "space", None), P()),
        check_vma=False,
    )
```

profile of v0, /device:TPU:12, one launch (start us, length us, event | category | flops | bytes accessed | tf_op | source)
XLA Modules:
  0.0 503.2 jit_solution(8383597021539726154)
XLA Ops:
  8.0 5.1 %fusion.68 = f32[2,18432]{1,0:T(2,128)S(1)} fusion(bf16[256,18432]{1,0:T(8,128)(2,1)} %param.21, bf16[2,128]{1,0:T(2,128)(2,1)S(1)} %get-tuple-element.260, bf16[2,128]{1,0:T(2,128)(2,1)S(1)} %get-tuple-element.259), kind=kOutput, calls=%fused_computation.113 | convolution fusion | flops 18876416 | bytes 9585664 | tf_op jit(solution)/shard_map/dot_general | solution.py:100
  16.0 4.4 slice_bitcast_fusion.5
  20.4 41.2 %all-gather.5.cloned.1.call-done = bf16[2,1,512,3072]{3,2,0,1:T(8,128)(2,1)} async-done(((bf16[2,1,64,3072]{3,2,0,1:T(8,128)(2,1)}), bf16[2,1,512,3072]{3,2,0,1:T(8,128)(2,1)}) %all-gather.5.cloned.1.call-update) | async-done | bytes 6291472 | tf_op jit(solution)/shard_map/all_gather | solution.py:106
  61.6 9.9 %fusion.52 = bf16[2,512,768]{2,1,0:T(8,128)(2,1)} fusion(bf16[3072,256]{1,0:T(8,128)(2,1)} %get-tuple-element.251, bf16[3072,256]{1,0:T(8,128)(2,1)} %get-tuple-element.252, bf16[3072,256]{1,0:T(8,128)(2,1)S(1)} %get-tuple-element.250, bf16[2,1,512,3072]{3,2,0,1:T(8,128)(2,1)} %all-gather.5.cloned.1.call-done), kind=kOutput, calls=%fused_computation.84 | convolution fusion | flops 4846780416 | bytes 12582912 | tf_op jit(solution)/shard_map/dot_general | solution.py:105
  71.4 12.7 %while.43 = (s32[]{:T(128)}, bf16[2,512,256]{2,1,0:T(8,128)(2,1)S(1)}, bf16[2,512,768]{2,1,0:T(8,128)(2,1)}, s32[2,16,16]{2,1,0:T(8,128)S(1)}, s32[2]{0:T(128)S(1)}, /*index=5*/s32[]{:T(128)}, s32[]{:T(128)}, s32[]{:T(128)}) while((s32[]{:T(128)}, bf16[2,512,256]{2,1,0:T(8,128)(2,1)S(1)}, bf16[2,512,768]{2,1,0:T(8,128)(2,1)}, ...), condition=%wide.region_7.8_spmd, body=%wide.region_2.7_spmd.sunk | while | flops 137174784 | bytes 10541854 | solution.py:119
  71.4 1.3 constant_dynamic-slice_fusion.4
  74.7 2.7 while.45
  81.0 2.7 while.45
  84.7 12.6 %all_to_all.30 = bf16[512,2,1,256]{3,1,2,0:T(2,128)(2,1)S(1)} all-to-all(bf16[512,2,1,256]{3,1,2,0:T(2,128)(2,1)S(1)} %bitcast.158), channel_id=1, replica_groups=mesh['frame'=4,'space'=8] {'space'}, dimensions={0} | all-to-all | bytes 1048576 | tf_op jit(solution)/shard_map/all_to_all | solution.py:124
  97.5 42.3 %all-gather.7.cloned.1.call-done = bf16[2048,3072]{1,0:T(8,128)(2,1)} async-done(((bf16[256,3072]{1,0:T(8,128)(2,1)}), bf16[2048,3072]{1,0:T(8,128)(2,1)}) %all-gather.7.cloned.1.call-update) | async-done | bytes 12582928 | tf_op jit(solution)/shard_map/all_gather | solution.py:123
  139.8 7.7 %convert_reduce_fusion = f32[128,3072]{1,0:T(8,128)} fusion(bf16[128,8,256]{2,0,1:T(8,128)(2,1)S(1)} %reshape_reshape.6, bf16[8,256,3072]{2,1,0:T(8,128)(2,1)} %bitcast.152), kind=kOutput, calls=%fused_computation.53 | convolution fusion | flops 1619656704 | bytes 14680064 | tf_op jit(solution)/shard_map/rgc,gcd->rgd/dot_general | solution.py:89
  147.5 2.2 reshape.315
  150.8 1.3 fusion.58
  152.7 6.7 %slice_bitcast_fusion.2 = (bf16[3072,512]{1,0:T(8,128)(2,1)}, bf16[3072,512]{1,0:T(8,128)(2,1)}, bf16[3072,512]{1,0:T(8,128)(2,1)}) fusion(bf16[3,3072,512]{2,1,0:T(8,128)(2,1)} %param.24), kind=kLoop, calls=%fused_computation.72 | loop fusion | bytes 18874368 | tf_op jit(solution)/shard_map/squeeze | solution.py:135
  159.5 54.6 %all-gather.9.cloned.1.call-done = bf16[2,4,64,3072]{3,2,0,1:T(8,128)(2,1)} async-done(((bf16[2,1,64,3072]{3,2,0,1:T(8,128)(2,1)}), bf16[2,4,64,3072]{3,2,0,1:T(8,128)(2,1)}) %all-gather.9.cloned.1.call-update) | async-done | bytes 3145744 | tf_op jit(solution)/shard_map/all_gather | solution.py:137
  214.0 9.7 %fusion.45 = bf16[2,4,64,1536]{3,2,1,0:T(8,128)(2,1)S(1)} fusion(bf16[3072,512]{1,0:T(8,128)(2,1)} %get-tuple-element.248, bf16[3072,512]{1,0:T(8,128)(2,1)} %get-tuple-element.249, bf16[3072,512]{1,0:T(8,128)(2,1)} %get-tuple-element.247, bf16[2,4,64,3072]{3,2,0,1:T(8,128)(2,1)} %all-gather.9.cloned.1.call-done), kind=kOutput, calls=%fused_computation.73 | convolution fusion | flops 4860936192 | bytes 14155776 | tf_op jit(solution)/shard_map/dot_general | solution.py:136
  223.7 11.9 %while.44 = (s32[]{:T(128)}, bf16[2,4,64,512]{3,2,0,1:T(8,128)(2,1)}, bf16[2,4,64,1536]{3,2,1,0:T(8,128)(2,1)S(1)}, s32[2]{0:T(128)S(1)}, s32[]{:T(128)}) while((s32[]{:T(128)}, bf16[2,4,64,512]{3,2,0,1:T(8,128)(2,1)}, bf16[2,4,64,1536]{3,2,1,0:T(8,128)(2,1)S(1)}, s32[2]{0:T(128)S(1)}, s32[]{:T(128)}) %tuple.106), condition=%wide.region_14.15_spmd, body=%wide.region_11.14_spmd.sunk | while | flops 2252841 | bytes 7479929 | solution.py:146
  224.7 1.4 fusion.109
  230.7 1.4 fusion.109
  235.6 6.2 %all-to-all-start.1 = ((bf16[4,2,64,512]{3,2,1,0:T(8,128)(2,1)}), bf16[4,2,64,512]{3,2,1,0:T(8,128)(2,1)S(1)}, u32[]{:S(2)}, u32[]{:S(2)}) async-start(bf16[4,2,64,512]{3,2,1,0:T(8,128)(2,1)} %bitcast.161), calls=%async_computation.1 | async-start | bytes 1048576 | tf_op jit(solution)/shard_map/all_to_all | solution.py:149
  243.1 198.7 %all-gather.11.cloned.1.call-done = bf16[2048,3072]{1,0:T(8,128)(2,1)} async-done(((bf16[512,3072]{1,0:T(8,128)(2,1)}), bf16[2048,3072]{1,0:T(8,128)(2,1)}) %all-gather.11.cloned.1.call-update) | async-done | bytes 12582928 | tf_op jit(solution)/shard_map/all_gather | solution.py:148
  441.8 6.6 %convert_reduce_fusion.1 = f32[128,3072]{1,0:T(8,128)S(1)} fusion(bf16[128,4,512]{2,0,1:T(8,128)(2,1)S(1)} %bitcast.157, bf16[4,512,3072]{2,1,0:T(8,128)(2,1)} %bitcast.153), kind=kOutput, calls=%fused_computation.62 | convolution fusion | flops 1614938112 | bytes 14680064 | tf_op jit(solution)/shard_map/rgc,gcd->rgd/dot_general | solution.py:89
  448.4 1.4 multiply_reduce_fusion
  450.5 44.4 %psum.7 = f32[]{:T(128)} all-reduce(f32[]{:T(128)} %fusion.67), channel_id=1, replica_groups=mesh['frame'=4,'space'=8] {'frame','space'}, use_global_device_ids=true, to_apply=%region_18.19 | all-reduce | flops 1 | bytes 8 | tf_op jit(solution)/shard_map/psum | solution.py:164
  (116 shorter events, 27.3 us)
Async XLA Ops:
  7.2 54.4 %all-gather.5.cloned.1.call-start = ((), (), s32[]{:S(2)}) async-start(), calls=%async_computation.2 | async-start | bytes 7077888 | tf_op jit(solution)/shard_map/all_gather | solution.py:106
  8.0 5.1 %copy-start = (bf16[2,1,64,3072]{3,2,1,0:T(8,128)(2,1)S(1)}, bf16[2,1,64,3072]{3,2,1,0:T(8,128)(2,1)}, u32[]{:S(2)}) copy-start(bf16[2,1,64,3072]{3,2,1,0:T(8,128)(2,1)} %param.16) | copy-start | bytes 2359300
  15.0 0.8 copy-start.3
  15.0 124.8 %all-gather.7.cloned.1.call-start = ((), (), s32[]{:S(2)}) async-start(), calls=%async_computation.3 | async-start | bytes 14155776 | tf_op jit(solution)/shard_map/all_gather | solution.py:123
  15.8 198.3 %all-gather.9.cloned.1.call-start = ((), (), s32[]{:S(2)}) async-start(), calls=%async_computation.4 | async-start | bytes 3932160 | tf_op jit(solution)/shard_map/all_gather | solution.py:137
  61.6 9.9 %copy-start.2 = (s32[2,16,16]{2,1,0:T(8,128)S(1)}, s32[2,16,16]{2,1,0:T(8,128)}, u32[]{:S(2)}) copy-start(s32[2,16,16]{2,1,0:T(8,128)} %param.20) | copy-start | bytes 6148
  152.1 289.7 %all-gather.11.cloned.1.call-start = ((), (), s32[]{:S(2)}) async-start(), calls=%async_computation.5 | async-start | bytes 15728640 | tf_op jit(solution)/shard_map/all_gather | solution.py:148
  235.6 206.2 %all-to-all-start.1 = ((bf16[4,2,64,512]{3,2,1,0:T(8,128)(2,1)}), bf16[4,2,64,512]{3,2,1,0:T(8,128)(2,1)S(1)}, u32[]{:S(2)}, u32[]{:S(2)}) async-start(bf16[4,2,64,512]{3,2,1,0:T(8,128)(2,1)} %bitcast.161), calls=%async_computation.1 | async-start | bytes 1048576 | tf_op jit(solution)/shard_map/all_to_all | solution.py:149
  441.8 6.6 %copy-start.1 = (bf16[2,1,64,3072]{3,2,1,0:T(8,128)(2,1)S(1)}, bf16[2,1,64,3072]{3,2,1,0:T(8,128)(2,1)}, u32[]{:S(2)}) copy-start(bf16[2,1,64,3072]{3,2,1,0:T(8,128)(2,1)} %param.17) | copy-start | bytes 2359300
Sparse Core Ops, SparseCore 0:
  15.1 46.3 all-gather.4
  63.5 76.3 all-gather.6
  152.2 61.7 all-gather.8
  215.5 226.2 all-gather.10
where the time goes:
time: 504 us; the launch traced here: 503 us
  waiting for transfers between devices  338 us (67%)
  blocking collectives  57 us (11%)
  matrix products  45.9 us (9%)
  local copies, waits for them, and re-layouts  26.5 us (5%)
  between operations  16.3 us (3%)
  other arithmetic  12.6 us (2%)
  starting transfers between devices  6.4 us (1%)
    all_gather x1, waiting for transfers between devices, shards(): w_tall = lax.all_gather(w_tout, 'frame', axis=0, tiled=True)  199 us
    all_gather x1, waiting for transfers between devices, shards(): lax.all_gather(h_two, 'frame', axis=1, tiled=True)  54.6 us
    psum x1, blocking collectives, shards(): total = lax.psum(local_total, ('frame', 'space'))  44.4 us
    all_gather x1, waiting for transfers between devices, shards(): w_sall = lax.all_gather(w_sout, 'space', axis=0, tiled=True)  42.3 us
    all_gather x1, waiting for transfers between devices, shards(): lax.all_gather(h_one, 'space', axis=2, tiled=True)  41.2 us
    dot_general x2, matrix products, group_project(): jnp.einsum('rgc,gcd->rgd', parts, weights, preferred_element_type=jnp.flo...  14.3 us
    all_to_all x1, blocking collectives, shards(): lax.all_to_all(spatial_att, 'space', split_axis=0, concat_axis=3, tiled=T...  12.6 us
  transfers between devices with their start and end apart: 5, of which 4 were waited for; matrix products, arithmetic and copies ran while one was open for 11% of the time, Pallas kernels for 0%

commit v1 on v0

--- a/solution.py
+++ b/solution.py
@@ -7,6 +7,28 @@
 HEAD_DIM = 128
 FREQ = 256
 TILE = 32
+
+
+def joined_along(blocks, dim):
+    shape = list(blocks.shape[1:])
+    shape[dim] *= blocks.shape[0]
+    return jnp.moveaxis(blocks, 0, dim).reshape(shape)
+
+
+def gather_around(x, axis, dim):
+    count = lax.axis_size(axis)
+    pairs = [(i, (i + 1) % count) for i in range(count)]
+    back = [(b, a) for a, b in pairs]
+    lower, upper = ([], [])
+    for hop in range(count - 1):
+        if hop % 2 == 0:
+            lower.append(lax.ppermute(lower[-1] if lower else x, axis, pairs))
+        else:
+            upper.append(lax.ppermute(upper[-1] if upper else x, axis, back))
+    blocks = jnp.stack([*lower[::-1], x, *upper])
+    shift = lax.axis_index(axis) - len(lower)
+    blocks = blocks[(jnp.arange(count) - shift) % count]
+    return joined_along(blocks, dim)
 
 
 def layer_norm(values):
@@ -145,7 +167,7 @@
 
     temporal_att = lax.map(per_video, (qkv_frame, valid[:, 0]))
     temporal_att = jnp.transpose(temporal_att, (1, 0, 2, 3))
-    w_tall = lax.all_gather(w_tout, "frame", axis=0, tiled=True)
+    w_tall = gather_around(w_tout, "frame", 0)
     own_frames = lax.all_to_all(temporal_att, "frame", split_axis=0, concat_axis=3, tiled=True)
     temporal = group_project(
         own_frames.reshape(frames_dev * videos * span_dev, -1), w_tall, frame_count

time: 504 us -> 487 us (0.966)
  waiting for transfers between devices: 338 us -> 267 us
  local copies, waits for them, and re-layouts: 26.5 us -> 69.6 us
  blocking collectives: 57 us -> 41.5 us
  starting transfers between devices: 6.4 us -> 20.1 us
  other arithmetic: 12.6 us -> 24.1 us
    all_gather x1 -> x0, waiting for transfers between devices: 199 us -> none  [shards(): w_tall = lax.all_gather(w_tout, 'frame', axis=0, tiled=True)]
    ppermute x0 -> x3, waiting for transfers between devices: none -> 181 us  [the longest x1 115 us: gather_around(): upper.append(lax.ppermute(upper[-1] if upper else x, axis, back))]
    all_gather x1, waiting for transfers between devices: 54.6 us -> 0.01 us  [shards(): lax.all_gather(h_two, 'frame', axis=1, tiled=True)]
    gather x0 -> x5, local copies, waits for them, and re-layouts: none -> 40.3 us  [gather_around(): blocks = blocks[(jnp.arange(count) - shift) % count]]
    all_to_all x1 -> x0, blocking collectives: 12.6 us -> none  [shards(): lax.all_to_all(spatial_att, 'space', split_axis=0, concat_axis=3, tiled=T...]
    ppermute x0 -> x3, starting transfers between devices: none -> 9.96 us  [the longest x2 9.37 us: gather_around(): lower.append(lax.ppermute(lower[-1] if lower else x, axis, pairs))]
    another operation x3 -> x4, other arithmetic: 0.11 us -> 9.65 us  [the longest x1 9.53 us: gather_around(): blocks = jnp.stack([*lower[::-1], x, *upper])]
    all_to_all x0 -> x1, waiting for transfers between devices: none -> 6.79 us  [shards(): lax.all_to_all(spatial_att, 'space', split_axis=0, concat_axis=3, tiled=T...]
  transfers between devices with their start and end apart: 5 -> 8, of which waited for: 4 -> 6; matrix products, arithmetic and copies ran while one was open for 11% -> 20% of each run, Pallas kernels for 0% -> 0%
where the time goes in v1:
time: 487 us; the launch traced here: 485 us
  waiting for transfers between devices  267 us (55%)
  local copies, waits for them, and re-layouts  69.6 us (14%)
  matrix products  45.8 us (9%)
  blocking collectives  41.5 us (9%)
  other arithmetic  24.1 us (5%)
  starting transfers between devices  20.1 us (4%)
  between operations  16.3 us (3%)
    ppermute x1, waiting for transfers between devices, gather_around(): upper.append(lax.ppermute(upper[-1] if upper else x, axis, back))  115 us
    ppermute x2, waiting for transfers between devices, gather_around(): lower.append(lax.ppermute(lower[-1] if lower else x, axis, pairs))  66.5 us
    psum x1, blocking collectives, shards(): total = lax.psum(local_total, ('frame', 'space'))  41.5 us
    all_gather x1, waiting for transfers between devices, shards(): lax.all_gather(h_one, 'space', axis=2, tiled=True)  41.2 us
    gather x5, local copies, waits for them, and re-layouts, gather_around(): blocks = blocks[(jnp.arange(count) - shift) % count]  40.3 us
    all_gather x1, waiting for transfers between devices, shards(): w_sall = lax.all_gather(w_sout, 'space', axis=0, tiled=True)  37.2 us
    dot_general x2, matrix products, group_project(): jnp.einsum('rgc,gcd->rgd', parts, weights, preferred_element_type=jnp.flo...  14.2 us
    dot_general x1, matrix products, shards(): jnp.dot(lax.all_gather(h_one, 'space', axis=2, tiled=True), w_flat, prefe...  9.87 us
  transfers between devices with their start and end apart: 8, of which 6 were waited for; matrix products, arithmetic and copies ran while one was open for 20% of the time, Pallas kernels for 0%

profile of v1, /device:TPU:12, one launch (start us, length us, event | category | flops | bytes accessed | tf_op | source)
XLA Modules:
  0.0 484.8 jit_solution(7611240742492585446)
XLA Ops:
  8.0 5.1 %fusion.77 = f32[2,18432]{1,0:T(2,128)S(1)} fusion(bf16[256,18432]{1,0:T(8,128)(2,1)} %param.21, bf16[2,128]{1,0:T(2,128)(2,1)S(1)} %get-tuple-element.262, bf16[2,128]{1,0:T(2,128)(2,1)S(1)} %get-tuple-element.261), kind=kOutput, calls=%fused_computation.125 | convolution fusion | flops 18876416 | bytes 9585664 | tf_op jit(solution)/shard_map/dot_general | solution.py:122
  16.5 4.4 slice_bitcast_fusion.5
  20.9 41.2 %all-gather.4.cloned.1.call-done = bf16[2,1,512,3072]{3,2,0,1:T(8,128)(2,1)} async-done(((bf16[2,1,64,3072]{3,2,0,1:T(8,128)(2,1)}), bf16[2,1,512,3072]{3,2,0,1:T(8,128)(2,1)}) %all-gather.4.cloned.1.call-update) | async-done | bytes 6291472 | tf_op jit(solution)/shard_map/all_gather | solution.py:128
  62.2 9.9 %fusion.59 = bf16[2,512,768]{2,1,0:T(8,128)(2,1)} fusion(bf16[3072,256]{1,0:T(8,128)(2,1)} %get-tuple-element.253, bf16[3072,256]{1,0:T(8,128)(2,1)} %get-tuple-element.254, bf16[3072,256]{1,0:T(8,128)(2,1)S(1)} %get-tuple-element.252, bf16[2,1,512,3072]{3,2,0,1:T(8,128)(2,1)} %all-gather.4.cloned.1.call-done), kind=kOutput, calls=%fused_computation.91 | convolution fusion | flops 4846780416 | bytes 12582912 | tf_op jit(solution)/shard_map/dot_general | solution.py:127
  72.0 12.7 %while.43 = (s32[]{:T(128)}, bf16[2,512,256]{2,1,0:T(8,128)(2,1)S(1)}, bf16[2,512,768]{2,1,0:T(8,128)(2,1)}, s32[2,16,16]{2,1,0:T(8,128)S(1)}, s32[2]{0:T(128)S(1)}, /*index=5*/s32[]{:T(128)}, s32[]{:T(128)}, s32[]{:T(128)}) while((s32[]{:T(128)}, bf16[2,512,256]{2,1,0:T(8,128)(2,1)S(1)}, bf16[2,512,768]{2,1,0:T(8,128)(2,1)}, ...), condition=%wide.region_7.8_spmd, body=%wide.region_2.7_spmd.sunk | while | flops 137174784 | bytes 10541854 | solution.py:141
  91.8 6.8 %all-to-all-done = bf16[512,2,1,256]{3,1,2,0:T(2,128)(2,1)S(1)} async-done(((bf16[512,2,1,256]{3,1,2,0:T(2,128)(2,1)}), bf16[512,2,1,256]{3,1,2,0:T(2,128)(2,1)S(1)}, u32[]{:S(2)}, u32[]{:S(2)}) %all-to-all-start) | async-done | bytes 524320 | tf_op jit(solution)/shard_map/all_to_all | solution.py:146
  98.8 37.2 %all-gather.6.cloned.1.call-done = bf16[2048,3072]{1,0:T(8,128)(2,1)} async-done(((bf16[256,3072]{1,0:T(8,128)(2,1)}), bf16[2048,3072]{1,0:T(8,128)(2,1)}) %all-gather.6.cloned.1.call-update) | async-done | bytes 12582928 | tf_op jit(solution)/shard_map/all_gather | solution.py:145
  136.0 6.5 %convert_reduce_fusion = f32[128,3072]{1,0:T(8,128)S(1)} fusion(bf16[128,8,256]{2,0,1:T(8,128)(2,1)S(1)} %reshape_reshape.6, bf16[8,256,3072]{2,1,0:T(8,128)(2,1)} %bitcast.157), kind=kOutput, calls=%fused_computation.60 | convolution fusion | flops 1619656704 | bytes 14680064 | tf_op jit(solution)/shard_map/rgc,gcd->rgd/dot_general | solution.py:111
  148.9 17.0 %collective-permute-done = bf16[512,3072]{1,0:T(8,128)(2,1)} collective-permute-done((bf16[512,3072]{1,0:T(8,128)(2,1)}, bf16[512,3072]{1,0:T(8,128)(2,1)}, u32[]{:S(2)}, u32[]{:S(2)}) %collective-permute-start) | collective-permute-done | bytes 3145760 | tf_op jit(solution)/shard_map/ppermute | solution.py:25
  165.9 7.9 %collective-permute-start.1 = (bf16[512,3072]{1,0:T(8,128)(2,1)}, bf16[512,3072]{1,0:T(8,128)(2,1)}, u32[]{:S(2)}, u32[]{:S(2)}) collective-permute-start(bf16[512,3072]{1,0:T(8,128)(2,1)} %collective-permute-done), channel_id=1, source_target_pairs={{0,8},{8,16},{16,24},{24,0},{1,9},{9,17},{17,25},{25,1},{2,10},{10... | collective-permute-start | bytes 9437192 | tf_op jit(solution)/shard_map/ppermute | solution.py:25
  175.1 7.0 %slice_bitcast_fusion.2 = (bf16[3072,512]{1,0:T(8,128)(2,1)}, bf16[3072,512]{1,0:T(8,128)(2,1)}, bf16[3072,512]{1,0:T(8,128)(2,1)}) fusion(bf16[3,3072,512]{2,1,0:T(8,128)(2,1)} %param.24), kind=kLoop, calls=%fused_computation.79 | loop fusion | bytes 18874368 | tf_op jit(solution)/shard_map/squeeze | solution.py:157
  182.1 114.6 %collective-permute-done.2 = bf16[512,3072]{1,0:T(8,128)(2,1)} collective-permute-done((bf16[512,3072]{1,0:T(8,128)(2,1)}, bf16[512,3072]{1,0:T(8,128)(2,1)}, u32[]{:S(2)}, u32[]{:S(2)}) %collective-permute-start.2) | collective-permute-done | bytes 3145760 | tf_op jit(solution)/shard_map/ppermute | solution.py:27
  296.7 49.5 %collective-permute-done.1 = bf16[512,3072]{1,0:T(8,128)(2,1)} collective-permute-done((bf16[512,3072]{1,0:T(8,128)(2,1)}, bf16[512,3072]{1,0:T(8,128)(2,1)}, u32[]{:S(2)}, u32[]{:S(2)}) %collective-permute-start.1) | collective-permute-done | bytes 3145760 | tf_op jit(solution)/shard_map/ppermute | solution.py:25
  346.1 9.5 %pad_maximum_fusion = bf16[4,512,3072]{2,1,0:T(8,128)(2,1)} fusion(bf16[1,512,3072]{2,1,0:T(8,128)(2,1)} %bitcast.28, bf16[1,512,3072]{2,1,0:T(8,128)(2,1)S(1)} %bitcast.161, bf16[1,512,3072]{2,1,0:T(8,128)(2,1)} %bitcast.26, bf16[1,512,3072]{2,1,0:T(8,128)(2,1)} %bitcast.25), kind=kLoop, calls=%fused_computation.55 | loop fusion | flops 18874368 | bytes 25165824 | tf_op jit(solution)/shard_map/stack | solution.py:28
  355.7 9.7 %fusion.52 = bf16[2,4,64,1536]{3,2,1,0:T(8,128)(2,1)S(1)} fusion(bf16[3072,512]{1,0:T(8,128)(2,1)} %get-tuple-element.250, bf16[3072,512]{1,0:T(8,128)(2,1)} %get-tuple-element.251, bf16[3072,512]{1,0:T(8,128)(2,1)} %get-tuple-element.249, bf16[2,4,64,3072]{3,2,0,1:T(8,128)(2,1)} %all-gather.8.cloned.1.call-done), kind=kOutput, calls=%fused_computation.80 | convolution fusion | flops 4860936192 | bytes 14155776 | tf_op jit(solution)/shard_map/dot_general | solution.py:158
  365.4 11.8 %while.44 = (s32[]{:T(128)}, bf16[2,4,64,512]{3,2,0,1:T(8,128)(2,1)}, bf16[2,4,64,1536]{3,2,1,0:T(8,128)(2,1)S(1)}, s32[2]{0:T(128)S(1)}, s32[]{:T(128)}) while((s32[]{:T(128)}, bf16[2,4,64,512]{3,2,0,1:T(8,128)(2,1)}, bf16[2,4,64,1536]{3,2,1,0:T(8,128)(2,1)S(1)}, s32[2]{0:T(128)S(1)}, s32[]{:T(128)}) %tuple.107), condition=%wide.region_14.15_spmd, body=%wide.region_11.14_spmd.sunk | while | flops 2252841 | bytes 7479929 | solution.py:168
  377.1 5.8 %all-to-all-start.1 = ((bf16[4,2,64,512]{3,2,1,0:T(8,128)(2,1)}), bf16[4,2,64,512]{3,2,1,0:T(8,128)(2,1)S(1)}, u32[]{:S(2)}, u32[]{:S(2)}) async-start(bf16[4,2,64,512]{3,2,1,0:T(8,128)(2,1)} %bitcast.165), calls=%async_computation.1 | async-start | bytes 1048576 | tf_op jit(solution)/shard_map/all_to_all | solution.py:171
  383.0 10.3 %fusion.93 = (bf16[4,512,1536]{2,1,0:T(8,128)(2,1)}, bf16[4,512,1536]{2,1,0:T(8,128)(2,1)}) fusion(bf16[4,512,3072]{2,1,0:T(8,128)(2,1)} %pad_maximum_fusion), kind=kLoop, calls=%fused_computation.148 | loop fusion | bytes 25165824 | tf_op jit(solution)/shard_map/gather | solution.py:30
  393.2 6.4 %gather_fusion = bf16[4,512,1536]{2,1,0:T(8,128)(2,1)} fusion(bf16[4,512,1536]{2,1,0:T(8,128)(2,1)} %get-tuple-element.247, s32[1024]{0:T(1024)S(1)} %pad_clamp_fusion), kind=kCustom, calls=%fused_computation | custom fusion | bytes 12582928 | tf_op jit(solution)/shard_map/gather | solution.py:30
  399.6 8.7 %copy.77 = bf16[4,512,1536]{1,2,0:T(8,128)(2,1)} copy(bf16[4,512,1536]{2,1,0:T(8,128)(2,1)} %gather_fusion) | data formatting | bytes 12582912 | tf_op jit(solution)/shard_map/gather | solution.py:30
  408.3 6.3 %gather_fusion.1 = bf16[4,512,1536]{2,1,0:T(8,128)(2,1)} fusion(bf16[4,512,1536]{2,1,0:T(8,128)(2,1)} %get-tuple-element.248, s32[1024]{0:T(1024)S(1)} %pad_clamp_fusion), kind=kCustom, calls=%fused_computation.1 | custom fusion | bytes 12582928 | tf_op jit(solution)/shard_map/gather | solution.py:30
  414.6 8.6 %copy.78 = bf16[4,512,1536]{1,2,0:T(8,128)(2,1)} copy(bf16[4,512,1536]{2,1,0:T(8,128)(2,1)} %gather_fusion.1) | data formatting | bytes 12582912 | tf_op jit(solution)/shard_map/gather | solution.py:30
  423.3 7.8 %convert_reduce_fusion.1 = f32[3072,128]{1,0:T(8,128)} fusion(bf16[128,4,512]{2,0,1:T(8,128)(2,1)S(1)} %bitcast.166, bf16[4,512,1536]{1,2,0:T(8,128)(2,1)} %copy.78, bf16[4,512,1536]{1,2,0:T(8,128)(2,1)} %copy.77), kind=kOutput, calls=%fused_computation.69 | convolution fusion | flops 1640103936 | bytes 14680064 | tf_op jit(solution)/shard_map/rgc,gcd->rgd/dot_general | solution.py:111
  435.0 41.5 %psum.7 = f32[]{:T(128)} all-reduce(f32[]{:T(128)} %fusion.76), channel_id=1, replica_groups=mesh['frame'=4,'space'=8] {'frame','space'}, use_global_device_ids=true, to_apply=%region_18.19 | all-reduce | flops 1 | bytes 8 | tf_op jit(solution)/shard_map/psum | solution.py:186
  (133 shorter events, 51.9 us)
Async XLA Ops:
  7.2 55.0 %all-gather.4.cloned.1.call-start = ((), (), s32[]{:S(2)}) async-start(), calls=%async_computation.2 | async-start | bytes 7077888 | tf_op jit(solution)/shard_map/all_gather | solution.py:128
  8.0 5.7 %copy-start = (bf16[2,1,64,3072]{3,2,1,0:T(8,128)(2,1)S(1)}, bf16[2,1,64,3072]{3,2,1,0:T(8,128)(2,1)}, u32[]{:S(2)}) copy-start(bf16[2,1,64,3072]{3,2,1,0:T(8,128)(2,1)} %param.16) | copy-start | bytes 2359300
  13.1 3.3 copy-start.5
  15.6 120.3 %all-gather.6.cloned.1.call-start = ((), (), s32[]{:S(2)}) async-start(), calls=%async_computation.3 | async-start | bytes 14155776 | tf_op jit(solution)/shard_map/all_gather | solution.py:145
  62.1 9.9 %copy-start.3 = (s32[2,16,16]{2,1,0:T(8,128)S(1)}, s32[2,16,16]{2,1,0:T(8,128)}, u32[]{:S(2)}) copy-start(s32[2,16,16]{2,1,0:T(8,128)} %param.20) | copy-start | bytes 6148
  86.1 12.5 %all-to-all-start = ((bf16[512,2,1,256]{3,1,2,0:T(2,128)(2,1)}), bf16[512,2,1,256]{3,1,2,0:T(2,128)(2,1)S(1)}, u32[]{:S(2)}, u32[]{:S(2)}) async-start(bf16[512,2,1,256]{3,1,2,0:T(2,128)(2,1)} %bitcast.119), calls=%async_computation | async-start | bytes 1048576 | tf_op jit(solution)/shard_map/all_to_all | solution.py:146
  90.3 265.4 %all-gather.8.cloned.1.call-start = ((), (), s32[]{:S(2)}) async-start(), calls=%async_computation.4 | async-start | bytes 3932160 | tf_op jit(solution)/shard_map/all_gather | solution.py:159
  90.3 75.6 %collective-permute-start = (bf16[512,3072]{1,0:T(8,128)(2,1)}, bf16[512,3072]{1,0:T(8,128)(2,1)}, u32[]{:S(2)}, u32[]{:S(2)}) collective-permute-start(bf16[512,3072]{1,0:T(8,128)(2,1)} %param.25), channel_id=1, source_target_pairs={{0,8},{8,16},{16,24},{24,0},{1,9},{9,17},{17,25},{25,1},{2,10},{10... | collective-permute-start | bytes 9437192 | tf_op jit(solution)/shard_map/ppermute | solution.py:25
  148.3 148.4 %collective-permute-start.2 = (bf16[512,3072]{1,0:T(8,128)(2,1)}, bf16[512,3072]{1,0:T(8,128)(2,1)}, u32[]{:S(2)}, u32[]{:S(2)}) collective-permute-start(bf16[512,3072]{1,0:T(8,128)(2,1)} %param.25), channel_id=1, source_target_pairs={{8,0},{16,8},{24,16},{0,24},{9,1},{17,9},{25,17},{1,25},{10,2},{18... | collective-permute-start | bytes 9437192 | tf_op jit(solution)/shard_map/ppermute | solution.py:27
  165.9 180.3 %collective-permute-start.1 = (bf16[512,3072]{1,0:T(8,128)(2,1)}, bf16[512,3072]{1,0:T(8,128)(2,1)}, u32[]{:S(2)}, u32[]{:S(2)}) collective-permute-start(bf16[512,3072]{1,0:T(8,128)(2,1)} %collective-permute-done), channel_id=1, source_target_pairs={{0,8},{8,16},{16,24},{24,0},{1,9},{9,17},{17,25},{25,1},{2,10},{10... | collective-permute-start | bytes 9437192 | tf_op jit(solution)/shard_map/ppermute | solution.py:25
  175.1 171.0 %copy-start.1 = (bf16[512,3072]{1,0:T(8,128)(2,1)S(1)}, bf16[512,3072]{1,0:T(8,128)(2,1)}, u32[]{:S(2)}) copy-start(bf16[512,3072]{1,0:T(8,128)(2,1)} %param.25) | copy-start | bytes 9437188
  377.1 46.1 %all-to-all-start.1 = ((bf16[4,2,64,512]{3,2,1,0:T(8,128)(2,1)}), bf16[4,2,64,512]{3,2,1,0:T(8,128)(2,1)S(1)}, u32[]{:S(2)}, u32[]{:S(2)}) async-start(bf16[4,2,64,512]{3,2,1,0:T(8,128)(2,1)} %bitcast.165), calls=%async_computation.1 | async-start | bytes 1048576 | tf_op jit(solution)/shard_map/all_to_all | solution.py:171
  431.0 2.0 copy-start.2
  431.0 2.0 copy-start.4
Sparse Core Ops, SparseCore 0:
  15.7 46.3 all-gather.3
  64.0 71.8 all-gather.5
  148.4 152.0 all-gather.7
